TPU v7x, 256 devices: a whole 4x4x8 slice. The times are simulated.
256 devices in a mesh: depth: 2 (over core), tile: 128 (over z, y, x).
Axes of the slice: x: 4, y: 4, z: 8, core: 2. Of those that a mesh axis runs over, the one named last changes fastest.
Arguments:
- transmission: float32 [2, 4, 8192, 2048], P(None, 'depth', 'tile'), may hold values from -1 to 1, as said below
- probe: float32 [2, 128, 128], replicated, may hold values from -4 to 4
- scan_rows: int32 [1024], P('tile'), may hold values from 0 to 8064, as said below
- scan_cols: int32 [1024], P('tile'), may hold values from 0 to 1920
- tile_counts: int32 [128], replicated, may hold values from 1 to 8, as said below
- diffraction: float32 [1024, 128, 128], P('tile'), may hold values from 0 to 2
Outputs:
- object_grad: float32 [2, 4, 8192, 2048], P(None, 'depth', 'tile')
- probe_grad: float32 [2, 128, 128], P(None, 'depth')
Inputs may be any that keep to these rules, and one draw needn't show every extreme that they name: `scan_rows`: slot i's row lies within [t * 64 - 128/2, t * 64 + 64 - 128/2) for t = i // 8, clipped to the specimen; both ends of the specimen are reached. `tile_counts`: some strip has all 8 slots filled and some strip only one. `transmission`: every entry has magnitude between 0.8 and 1.
All inputs are finite; a program needn't handle non-finite values.
Results may differ from a plain program's by a relative error of at most 0.0003.
Values sent between devices are 32-bit elements; how exact they have to be, the bound alone decides.
No kernel may reach another device: no remote copies, remote signals or barrier semaphores. Data moves between devices by JAX's collectives and lax.ppermute only.
A program may use at most 320 MiB of HBM per device.

v0:
```python
import math
import jax
import jax.numpy as jnp
from jax import lax
from jax.sharding import PartitionSpec as P

FRESNEL = 0.5
HIGH = lax.Precision.HIGHEST


def with_halo(value, sides, width):
    for axis, dim in sides:
        size, length = (lax.axis_size(axis), value.shape[dim])
        up = [(i, (i + 1) % size) for i in range(size - 1)]
        down = [(j, i) for i, j in up]
        last = lax.slice_in_dim(value, length - width, length, axis=dim)
        first = lax.slice_in_dim(value, 0, width, axis=dim)
        before = lax.ppermute(last, axis, up)
        after = lax.ppermute(first, axis, down)
        value = jnp.concatenate([before, value, after], axis=dim)
    return value


def shifted(value, axis, by):
    size = lax.axis_size(axis)
    pairs = [(i, i + by) for i in range(size) if 0 <= i + by < size]
    return lax.ppermute(value, axis, pairs)


def dft_tables(size):
    index = jnp.arange(size, dtype=jnp.int32)
    product = index[:, None] * index[None, :] % size
    angle = 2.0 * math.pi / size * product.astype(jnp.float32)
    scale = 1.0 / math.sqrt(size)
    cosine = jnp.cos(angle) * scale
    sine = jnp.sin(angle) * scale
    freq = ((index + size // 2) % size - size // 2).astype(jnp.float32)
    phase = FRESNEL * math.pi / size * (freq[:, None] ** 2 + freq[None, :] ** 2)
    return (cosine, sine, jnp.cos(phase), jnp.sin(phase))


def left_mul(real_m, imag_m, wave):
    wave_re = wave[..., 0, :, :]
    wave_im = wave[..., 1, :, :]

    def prod(m, x):
        return jnp.einsum("ij,...jk->...ik", m, x, precision=HIGH)

    return jnp.stack(
        [
            prod(real_m, wave_re) - prod(imag_m, wave_im),
            prod(real_m, wave_im) + prod(imag_m, wave_re),
        ],
        axis=-3,
    )


def right_mul(wave, real_m, imag_m):
    wave_re = wave[..., 0, :, :]
    wave_im = wave[..., 1, :, :]

    def prod(x, m):
        return jnp.einsum("...ij,jk->...ik", x, m, precision=HIGH)

    return jnp.stack(
        [
            prod(wave_re, real_m) - prod(wave_im, imag_m),
            prod(wave_re, imag_m) + prod(wave_im, real_m),
        ],
        axis=-3,
    )


def transform(wave, cosine, sine, sign):
    imag_m = sign * sine
    return right_mul(left_mul(cosine, imag_m, wave), cosine, imag_m)


def times(first, second):
    a_re, a_im = (first[..., 0, :, :], first[..., 1, :, :])
    b_re, b_im = (second[..., 0, :, :], second[..., 1, :, :])
    return jnp.stack([a_re * b_re - a_im * b_im, a_re * b_im + a_im * b_re], axis=-3)


def conj_times(first, second):
    a_re, a_im = (first[..., 0, :, :], first[..., 1, :, :])
    b_re, b_im = (second[..., 0, :, :], second[..., 1, :, :])
    return jnp.stack([a_re * b_re + a_im * b_im, a_re * b_im - a_im * b_re], axis=-3)


def propagate(wave, tables, adjoint):
    cosine, sine, kern_cos, kern_sin = tables
    spectrum = transform(wave, cosine, sine, -1.0)
    kernel = jnp.stack([kern_cos, kern_sin if adjoint else -kern_sin])
    return transform(times(kernel, spectrum), cosine, sine, 1.0)


def shards(transmission, probe, scan_rows, scan_cols, tile_counts, diffraction):
    size = probe.shape[-1]
    half = size // 2
    group = transmission.shape[1]
    strip = transmission.shape[2]
    slots = scan_rows.shape[0]
    tables = dft_tables(size)
    cosine, sine = (tables[0], tables[1])
    n_depth = lax.axis_size("depth")
    depth_pos = lax.axis_index("depth")
    tile_pos = lax.axis_index("tile")
    first = depth_pos == 0
    last = depth_pos == n_depth - 1
    filled = tile_counts[tile_pos]
    extended = with_halo(transmission, (("tile", 2),), half)
    local_rows = scan_rows - (tile_pos * strip - half)
    batch = 1
    offsets = jnp.arange(batch, dtype=jnp.int32)
    zero_index = jnp.int32(0)

    def cut(row, col):
        return lax.dynamic_slice(
            extended, (zero_index, zero_index, row, col), (2, group, size, size)
        )

    own_bank = jax.vmap(cut)(local_rows, scan_cols)

    def walk(wave, patches, finish):
        inputs = []
        for slice_pos in range(group):
            inputs.append(wave)
            if finish or slice_pos + 1 < group:
                wave = propagate(times(patches[:, :, slice_pos], wave), tables, False)
        return (wave, jnp.stack(inputs, axis=1))

    def seed_of(out_wave, measured):
        far = transform(out_wave, cosine, sine, -1.0)
        intensity = far[:, 0] ** 2 + far[:, 1] ** 2
        return transform((intensity - measured)[:, None] * far, cosine, sine, 1.0)

    grads_start = jnp.zeros(extended.shape, jnp.float32)
    order = jnp.arange(slots, dtype=jnp.int32)
    n_blocks = slots // batch
    count = order.shape[0]
    blocks = count // batch
    segments = n_blocks + n_depth - 1
    wave_shape = (batch, 2, size, size)

    def slot_state(block):
        positions = block * batch + offsets
        valid = (block >= 0) & (block < n_blocks) & (positions < filled)
        start = jnp.clip(block, 0, blocks - 1) * batch
        ids = order[start + offsets]
        return (valid, start, ids)

    saved_start = jnp.zeros((count, 2, size, size), jnp.float32)
    seeds_start = jnp.zeros((count, 2, size, size), jnp.float32)

    def forward_segment(step, state):
        incoming, saved, seeds = state
        valid, start, ids = slot_state(step - depth_pos)
        mask = valid.astype(jnp.float32)[:, None, None, None]
        wave = jnp.where(first, probe[None], incoming) * mask

        def forward_work(args):
            saved_in, seeds_in = args
            out_wave, inputs = walk(wave, jnp.take(own_bank, ids, axis=0), True)
            kept = inputs[:, 0]
            saved_out = lax.dynamic_update_slice_in_dim(saved_in, kept, start, 0)

            def write_seed(buffer):
                measured = jnp.take(diffraction, ids, axis=0)
                return lax.dynamic_update_slice_in_dim(
                    buffer, seed_of(out_wave, measured), start, 0
                )

            def leave_seed(buffer):
                return buffer

            seeds_out = lax.cond(last, write_seed, leave_seed, seeds_in)
            return (out_wave, saved_out, seeds_out)

        def forward_rest(args):
            return (jnp.zeros(wave_shape, jnp.float32), args[0], args[1])

        out_wave, saved, seeds = lax.cond(
            jnp.any(valid), forward_work, forward_rest, (saved, seeds)
        )
        incoming = shifted(out_wave, "depth", 1)
        return (incoming, saved, seeds)

    incoming0 = jnp.zeros(wave_shape, jnp.float32)
    _, saved, seeds = lax.fori_loop(
        0, segments, forward_segment, (incoming0, saved_start, seeds_start)
    )

    def backward_segment(step, state):
        incoming, windows, probe_acc = state
        valid, start, ids = slot_state(step - (n_depth - 1 - depth_pos))
        mask = valid.astype(jnp.float32)[:, None, None, None]
        arriving = (
            jnp.where(last, lax.dynamic_slice_in_dim(seeds, start, batch, 0), incoming) * mask
        )

        def backward_work(args):
            windows_in, probe_in = args
            patches = jnp.take(own_bank, ids, axis=0)
            _, inputs = walk(lax.dynamic_slice_in_dim(saved, start, batch, 0), patches, False)
            flow = arriving
            pieces = [None] * group
            for slice_pos in reversed(range(group)):
                along = propagate(flow, tables, True)
                pieces[slice_pos] = conj_times(inputs[:, slice_pos], along)
                flow = conj_times(patches[:, :, slice_pos], along)
            update = (
                jnp.stack(pieces, axis=2) * valid.astype(jnp.float32)[:, None, None, None, None]
            )
            windows_out = lax.dynamic_update_slice_in_dim(windows_in, update, start, 0)
            probe_out = probe_in + jnp.where(first, jnp.sum(flow * mask, axis=0), 0.0)
            return (flow, windows_out, probe_out)

        def backward_rest(args):
            return (jnp.zeros(wave_shape, jnp.float32), args[0], args[1])

        out_wave, windows, probe_acc = lax.cond(
            jnp.any(valid), backward_work, backward_rest, (windows, probe_acc)
        )
        incoming = shifted(out_wave, "depth", -1)
        return (incoming, windows, probe_acc)

    windows_start = jnp.zeros((count, 2, group, size, size), jnp.float32)
    probe_start = jnp.zeros(probe.shape, jnp.float32)
    _, windows, probe_acc = lax.fori_loop(
        0, segments, backward_segment, (incoming0, windows_start, probe_start)
    )
    windows, probe_acc = (windows, probe_acc)
    weights = jnp.ones((slots,), jnp.float32)

    def place_one(item, total):
        slot_id = order[item]
        place = (zero_index, zero_index, local_rows[slot_id], scan_cols[slot_id])
        current = lax.dynamic_slice(total, place, (2, group, size, size))
        return lax.dynamic_update_slice(total, current + windows[item] * weights[item], place)

    grads = lax.fori_loop(0, order.shape[0], place_one, grads_start)
    rims = jnp.concatenate([grads[:, :, :half], grads[:, :, half + strip :]], axis=2)
    arrived = with_halo(rims, (("tile", 2),), half)
    own = grads[:, :, half : half + strip]
    own = own.at[:, :, :half].add(arrived[:, :, :half])
    own = own.at[:, :, strip - half :].add(arrived[:, :, 3 * half :])
    probe_rows = lax.psum_scatter(probe_acc, "depth", scatter_dimension=1, tiled=True)
    probe_grad = lax.psum(probe_rows, "tile")
    return (own, probe_grad)


def solution(mesh):
    placed = (P(None, "depth", "tile", None), P(), P("tile"), P("tile"), P(), P("tile", None, None))
    return jax.shard_map(
        shards,
        mesh=mesh,
        in_specs=placed,
        out_specs=(P(None, "depth", "tile", None), P(None, "depth", None)),
        check_vma=False,
    )
```

profile of v0, /device:TPU:2, one launch (start us, length us, event | category | flops | bytes accessed | tf_op | source)
XLA Modules:
  0.0 889.9 jit_solution(7273562203496722747)
XLA Ops:
  15.8 40.8 %collective-permute-done.2 = f32[2,2,64,2048]{3,2,1,0:T(8,128)S(1)} collective-permute-done((f32[2,2,64,2048]{3,2,1,0:T(8,128)}, f32[2,2,64,2048]{3,2,1,0:T(8,128)S(1)}, u32[]{:S(2)}, u32[]{:S(2)}) %collective-permute-start.2) | collective-permute-done | bytes 2097184 | tf_op jit(solution)/shard_map/ppermute | solution.py:18
  59.9 5.7 pad_maximum_fusion.2
  65.8 24.3 %while.68 = (s32[]{:T(128)}, f32[2,2,192,2048]{3,2,1,0:T(8,128)}, s32[8,4]{0,1:T(4,128)S(1)}, f32[8,2,2,128,128]{4,3,1,2,0:T(8,128)S(1)}, s32[]{:T(128)}) while((s32[]{:T(128)}, f32[2,2,192,2048]{3,2,1,0:T(8,128)}, s32[8,4]{0,1:T(4,128)S(1)}, f32[8,2,2,128,128]{4,3,1,2,0:T(8,128)S(1)}, s32[]{:T(128)}) %tuple.373), condition=%wide.while_cond.6, body=%wide.while_body.6.sunk | while | flops 2 | bytes 525937 | solution.py:119
  92.4 91.4 %while.69 = (s32[]{:T(128)}, f32[1,2,128,128]{3,2,1,0:T(8,128)S(1)}, f32[8,2,128,128]{3,2,1,0:T(8,128)}, f32[8,2,128,128]{3,2,1,0:T(8,128)}, s32[]{:T(128)}, /*i...) while((s32[]{:T(128)}, ...), condition=%wide.region_5.7_spmd.clone.clone.clone, body=%wide.region_0.6_spmd.clone.clone.clone.sunk | while | flops 1209614336 | bytes 16059241 | solution.py:190
  93.1 13.6 %conditional.12 = (f32[1,2,128,128]{3,2,1,0:T(8,128)S(1)}, f32[8,2,128,128]{3,2,1,0:T(8,128)}, f32[8,2,128,128]{3,2,1,0:T(8,128)}) conditional(s32[]{:T(128)} %bitcast.558, (f32[8,2,128,128]{3,2,1,0:T(8,128)}, f32[8,2,128,128]{3,2,1,0:T(8,128)}) %tuple.363, (s32[]{:T(128)}, s32[8]{0:T(128)S(1)}, f32[8,2,2,128,128]{4,3,1,2,0:T(8,128)S(1)}, ...), branch_computations={%region_1.1_spmd, %region_2.5_spmd.clone} | conditional | flops 1209352192 | bytes 15337401 | solution.py:183
  109.6 13.6 %conditional.12 = (f32[1,2,128,128]{3,2,1,0:T(8,128)S(1)}, f32[8,2,128,128]{3,2,1,0:T(8,128)}, f32[8,2,128,128]{3,2,1,0:T(8,128)}) conditional(s32[]{:T(128)} %bitcast.558, (f32[8,2,128,128]{3,2,1,0:T(8,128)}, f32[8,2,128,128]{3,2,1,0:T(8,128)}) %tuple.363, (s32[]{:T(128)}, s32[8]{0:T(128)S(1)}, f32[8,2,2,128,128]{4,3,1,2,0:T(8,128)S(1)}, ...), branch_computations={%region_1.1_spmd, %region_2.5_spmd.clone} | conditional | flops 1209352192 | bytes 15337401 | solution.py:183
  123.2 10.3 %collective-permute-start = (f32[1,2,128,128]{3,2,1,0:T(8,128)S(1)}, f32[1,2,128,128]{3,2,1,0:T(8,128)S(1)}, u32[]{:S(2)}, u32[]{:S(2)}) collective-permute-start(f32[1,2,128,128]{3,2,1,0:T(8,128)S(1)} %get-tuple-element.2643), channel_id=1, source_target_pairs={{0,128},{1,129},{2,130},{3,131},{4,132},{5,133},{6,134},{7,135},{8... | collective-permute-start | bytes 393224 | tf_op jit(solution)/shard_map/while/body/eval_jaxpr/ppermute | solution.py:27
  135.2 23.9 %collective-permute-start = (f32[1,2,128,128]{3,2,1,0:T(8,128)S(1)}, f32[1,2,128,128]{3,2,1,0:T(8,128)S(1)}, u32[]{:S(2)}, u32[]{:S(2)}) collective-permute-start(f32[1,2,128,128]{3,2,1,0:T(8,128)S(1)} %get-tuple-element.2643), channel_id=1, source_target_pairs={{0,128},{1,129},{2,130},{3,131},{4,132},{5,133},{6,134},{7,135},{8... | collective-permute-start | bytes 393224 | tf_op jit(solution)/shard_map/while/body/eval_jaxpr/ppermute | solution.py:27
  185.4 94.9 %while.70 = (s32[]{:T(128)}, f32[1,2,128,128]{3,2,1,0:T(8,128)S(1)}, f32[8,2,2,128,128]{4,3,1,2,0:T(8,128)}, f32[2,128,128]{2,1,0:T(8,128)S(1)}, s32[]{:T(128)},...) while((s32[]{:T(128)}, ...), condition=%wide.region_9.11_spmd.clone.clone.clone, body=%wide.region_6.10_spmd.clone.clone.clone.sunk | while | flops 1210138624 | bytes 17565816 | solution.py:230
  187.6 21.1 %collective-permute-done.1 = f32[1,2,128,128]{3,2,1,0:T(8,128)S(1)} collective-permute-done((f32[1,2,128,128]{3,2,1,0:T(8,128)S(1)}, f32[1,2,128,128]{3,2,1,0:T(8,128)S(1)}, u32[]{:S(2)}, u32[]{:S(2)}) %collective-permute-start.1) | collective-permute-done | bytes 131104 | tf_op jit(solution)/shard_map/while/body/eval_jaxpr/ppermute | solution.py:27
  209.3 20.0 %conditional.13 = (f32[1,2,128,128]{3,2,1,0:T(8,128)S(1)}, f32[8,2,2,128,128]{4,3,1,2,0:T(8,128)}, f32[2,128,128]{2,1,0:T(8,128)S(1)}) conditional(s32[]{:T(128)} %bitcast.561, (f32[8,2,2,128,128]{4,3,1,2,0:T(8,128)}, f32[2,128,128]{2,1,0:T(8,128)S(1)}) %tuple.367, (s32[]{:T(128)}, s32[8]{0:T(128)S(1)}, f32[8,2,2,128,128]{4,3,1,2,0:T(8,128)S(1)}, ...), branch_computations={%region_7.8_spmd, %region_8.9_spmd.clone} | conditional | flops 1209876480 | bytes 16843968 | solution.py:222
  233.2 20.0 %conditional.13 = (f32[1,2,128,128]{3,2,1,0:T(8,128)S(1)}, f32[8,2,2,128,128]{4,3,1,2,0:T(8,128)}, f32[2,128,128]{2,1,0:T(8,128)S(1)}) conditional(s32[]{:T(128)} %bitcast.561, (f32[8,2,2,128,128]{4,3,1,2,0:T(8,128)}, f32[2,128,128]{2,1,0:T(8,128)S(1)}) %tuple.367, (s32[]{:T(128)}, s32[8]{0:T(128)S(1)}, f32[8,2,2,128,128]{4,3,1,2,0:T(8,128)S(1)}, ...), branch_computations={%region_7.8_spmd, %region_8.9_spmd.clone} | conditional | flops 1209876480 | bytes 16843968 | solution.py:222
  283.7 103.7 %while.67 = (s32[]{:T(128)}, f32[2,2,192,2048]{3,2,1,0:T(8,128)}, s32[8]{0:T(128)S(1)}, s32[8]{0:T(128)S(1)}, s32[8]{0:T(128)S(1)}, /*index=5*/f32[8,2,2,128,128...) while((s32[]{:T(128)}, f32[2,2,192,2048]{3,2,1,0:T(8,128)}, ...), condition=%wide.region_11.13_spmd, body=%wide.region_10.12_spmd.sunk | while | flops 65547 | bytes 1311491 | solution.py:242
  305.4 4.1 dynamic_update_slice.29
  318.3 4.1 dynamic_update_slice.29
  344.1 4.2 dynamic_update_slice.29
  357.1 4.1 dynamic_update_slice.29
  370.0 4.2 dynamic_update_slice.29
  383.1 4.3 dynamic_update_slice.29
  387.4 4.8 fusion.137
  392.2 86.4 %collective-permute-start.4 = (f32[2,2,64,2048]{3,2,1,0:T(8,128)}, f32[2,2,64,2048]{3,2,1,0:T(8,128)S(1)}, u32[]{:S(2)}, u32[]{:S(2)}) collective-permute-start(f32[2,2,64,2048]{3,2,1,0:T(8,128)} %get-tuple-element.2429), channel_id=1, source_target_pairs={{0,1},{1,2},{2,3},{3,4},{4,5},{5,6},{6,7},{7,8},{8,9},{9,10},{10,1... | collective-permute-start | bytes 6291464 | tf_op jit(solution)/shard_map/ppermute | solution.py:18
  480.6 181.8 %reduce-scatter.2.cloned.1.call-done = f32[2,64,128]{2,1,0:T(8,128)} async-done(((f32[2,128,128]{2,1,0:T(8,128)}), f32[2,64,128]{2,1,0:T(8,128)}) %reduce-scatter.2.cloned.1.call-update) | async-done | bytes 65552 | tf_op jit(solution)/shard_map/reduce_scatter | solution.py:248
  662.4 4.2 add_add_fusion
  666.6 215.0 %all-reduce.2.cloned.1.call-done = f32[2,64,128]{2,1,0:T(8,128)} async-done(((f32[2,64,128]{2,1,0:T(8,128)}), f32[2,64,128]{2,1,0:T(8,128)}) %all-reduce.2.cloned.1.call-update) | async-done | bytes 65552 | tf_op jit(solution)/shard_map/psum | solution.py:249
  (408 shorter events, 192.3 us)
Async XLA Ops:
  7.2 655.2 %reduce-scatter.2.cloned.1.call-start = ((), (), s32[]{:S(2)}) async-start(), calls=%async_computation.1 | async-start | bytes 196608 | tf_op jit(solution)/shard_map/reduce_scatter | solution.py:248
  7.2 49.5 %collective-permute-start.2 = (f32[2,2,64,2048]{3,2,1,0:T(8,128)}, f32[2,2,64,2048]{3,2,1,0:T(8,128)S(1)}, u32[]{:S(2)}, u32[]{:S(2)}) collective-permute-start(f32[2,2,64,2048]{3,2,1,0:T(8,128)} %param.28), channel_id=1, source_target_pairs={{0,1},{1,2},{2,3},{3,4},{4,5},{5,6},{6,7},{7,8},{8,9},{9,10},{10,1... | collective-permute-start | bytes 6291464 | tf_op jit(solution)/shard_map/ppermute | solution.py:18
  10.6 49.3 %collective-permute-start.3 = (f32[2,2,64,2048]{3,2,1,0:T(8,128)}, f32[2,2,64,2048]{3,2,1,0:T(8,128)}, u32[]{:S(2)}, u32[]{:S(2)}) collective-permute-start(f32[2,2,64,2048]{3,2,1,0:T(8,128)} %param.28), channel_id=1, source_target_pairs={{1,0},{2,1},{3,2},{4,3},{5,4},{6,5},{7,6},{8,7},{9,8},{10,9},{11,1... | collective-permute-start | bytes 6291464 | tf_op jit(solution)/shard_map/ppermute | solution.py:19
  106.7 2.3 collective-permute-start
  123.2 11.3 %collective-permute-start = (f32[1,2,128,128]{3,2,1,0:T(8,128)S(1)}, f32[1,2,128,128]{3,2,1,0:T(8,128)S(1)}, u32[]{:S(2)}, u32[]{:S(2)}) collective-permute-start(f32[1,2,128,128]{3,2,1,0:T(8,128)S(1)} %get-tuple-element.2643), channel_id=1, source_target_pairs={{0,128},{1,129},{2,130},{3,131},{4,132},{5,133},{6,134},{7,135},{8... | collective-permute-start | bytes 393224 | tf_op jit(solution)/shard_map/while/body/eval_jaxpr/ppermute | solution.py:27
  135.2 24.8 %collective-permute-start = (f32[1,2,128,128]{3,2,1,0:T(8,128)S(1)}, f32[1,2,128,128]{3,2,1,0:T(8,128)S(1)}, u32[]{:S(2)}, u32[]{:S(2)}) collective-permute-start(f32[1,2,128,128]{3,2,1,0:T(8,128)S(1)} %get-tuple-element.2643), channel_id=1, source_target_pairs={{0,128},{1,129},{2,130},{3,131},{4,132},{5,133},{6,134},{7,135},{8... | collective-permute-start | bytes 393224 | tf_op jit(solution)/shard_map/while/body/eval_jaxpr/ppermute | solution.py:27
  160.7 3.2 collective-permute-start
  164.7 3.2 collective-permute-start
  168.6 3.2 collective-permute-start
  172.6 3.2 collective-permute-start
  176.6 3.2 collective-permute-start
  180.5 3.2 collective-permute-start
  186.3 22.4 %collective-permute-start.1 = (f32[1,2,128,128]{3,2,1,0:T(8,128)S(1)}, f32[1,2,128,128]{3,2,1,0:T(8,128)S(1)}, u32[]{:S(2)}, u32[]{:S(2)}) collective-permute-start(f32[1,2,128,128]{3,2,1,0:T(8,128)S(1)} %get-tuple-element.2660), channel_id=1, source_target_pairs={{128,0},{129,1},{130,2},{131,3},{132,4},{133,5},{134,6},{135,7},{1... | collective-permute-start | bytes 393224 | tf_op jit(solution)/shard_map/while/body/eval_jaxpr/ppermute | solution.py:27
  229.3 3.2 collective-permute-start.1
  253.2 3.2 collective-permute-start.1
  257.2 3.2 collective-permute-start.1
  261.1 3.2 collective-permute-start.1
  265.1 3.2 collective-permute-start.1
  269.1 3.2 collective-permute-start.1
  273.0 3.2 collective-permute-start.1
  277.0 3.2 collective-permute-start.1
  392.2 270.3 %collective-permute-start.4 = (f32[2,2,64,2048]{3,2,1,0:T(8,128)}, f32[2,2,64,2048]{3,2,1,0:T(8,128)S(1)}, u32[]{:S(2)}, u32[]{:S(2)}) collective-permute-start(f32[2,2,64,2048]{3,2,1,0:T(8,128)} %get-tuple-element.2429), channel_id=1, source_target_pairs={{0,1},{1,2},{2,3},{3,4},{4,5},{5,6},{6,7},{7,8},{8,9},{9,10},{10,1... | collective-permute-start | bytes 6291464 | tf_op jit(solution)/shard_map/ppermute | solution.py:18
  478.6 183.9 %collective-permute-start.5 = (f32[2,2,64,2048]{3,2,1,0:T(8,128)}, f32[2,2,64,2048]{3,2,1,0:T(8,128)}, u32[]{:S(2)}, u32[]{:S(2)}) collective-permute-start(f32[2,2,64,2048]{3,2,1,0:T(8,128)} %get-tuple-element.2430), channel_id=1, source_target_pairs={{1,0},{2,1},{3,2},{4,3},{5,4},{6,5},{7,6},{8,7},{9,8},{10,9},{11,1... | collective-permute-start | bytes 6291464 | tf_op jit(solution)/shard_map/ppermute | solution.py:19
  480.5 401.1 %all-reduce.2.cloned.1.call-start = ((), (), s32[]{:S(2)}) async-start(), calls=%async_computation.2 | async-start | bytes 131072 | tf_op jit(solution)/shard_map/psum | solution.py:249
  (3 other events, 33.5 us)
Sparse Core Ops, SparseCore 0:
  480.6 181.7 reduce-scatter.1
  667.8 213.7 all-reduce.1
where the time goes:
time: 894 us; the launch traced here: 890 us
  waiting for transfers between devices  486 us (54%)
  starting transfers between devices  155 us (17%)
  local copies, waits for them, and re-layouts  91.8 us (10%)
  loops' own time  65.1 us (7%)
  matrix products  47.9 us (5%)
  other arithmetic  29.7 us (3%)
  between operations  14.2 us (2%)
    psum x1, waiting for transfers between devices, shards(): probe_grad = lax.psum(probe_rows, 'tile')  215 us
    reduce_scatter x1, waiting for transfers between devices, shards(): lax.psum_scatter(probe_acc, 'depth', scatter_dimension=1, tiled=True)  182 us
    ppermute x2, starting transfers between devices, with_halo(): before = lax.ppermute(last, axis, up)  89.8 us
    ppermute x18, starting transfers between devices, shifted(): return lax.ppermute(value, axis, pairs)  60.8 us
    ppermute x18, waiting for transfers between devices, shifted(): return lax.ppermute(value, axis, pairs)  45.2 us
    another operation x1, loops' own time, shards(): grads = lax.fori_loop(0, order.shape[0], place_one, grads_start)  44.9 us
    ppermute x2, waiting for transfers between devices, with_halo(): before = lax.ppermute(last, axis, up)  40.8 us
    dynamic_update_slice x8, local copies, waits for them, and re-layouts, place_one(): lax.dynamic_update_slice(total, current + windows[item] * weights[item],...  33 us
  transfers between devices with their start and end apart: 24, of which 22 were waited for; matrix products, arithmetic and copies ran while one was open for 1% of the time, Pallas kernels for 0%

commit v1 on v0

--- a/solution.py
+++ b/solution.py
@@ -246,7 +246,7 @@
     own = own.at[:, :, :half].add(arrived[:, :, :half])
     own = own.at[:, :, strip - half :].add(arrived[:, :, 3 * half :])
     probe_rows = lax.psum_scatter(probe_acc, "depth", scatter_dimension=1, tiled=True)
-    probe_grad = lax.psum(probe_rows, "tile")
+    probe_grad = jnp.sum(lax.all_gather(probe_rows, "tile"), axis=0)
     return (own, probe_grad)
 
 

time: 894 us -> 735 us (0.82); the launches traced: 890 us -> 721 us
  waiting for transfers between devices: 486 us -> 397 us
  starting transfers between devices: 155 us -> 72.8 us
    psum x1 -> x0, waiting for transfers between devices: 215 us -> none  [shards(): probe_grad = lax.psum(probe_rows, 'tile')]
    ppermute x2, starting transfers between devices: 89.8 us -> 7.15 us  [with_halo(): before = lax.ppermute(last, axis, up)]
    reduce_scatter x1, waiting for transfers between devices: 182 us -> 260 us  [shards(): lax.psum_scatter(probe_acc, 'depth', scatter_dimension=1, tiled=True)]
    ppermute x2, waiting for transfers between devices: 40.8 us -> 86.6 us  [with_halo(): before = lax.ppermute(last, axis, up)]
  transfers between devices with their start and end apart: 24 -> 24, of which waited for: 22 -> 23; matrix products, arithmetic and copies ran while one was open for 1% -> 10% of each run, Pallas kernels for 0% -> 0%
where the time goes in v1:
time: 735 us; the launch traced here: 721 us
  waiting for transfers between devices  397 us (54%)
  local copies, waits for them, and re-layouts  87.8 us (12%)
  starting transfers between devices  72.8 us (10%)
  loops' own time  68.4 us (9%)
  matrix products  47.9 us (7%)
  other arithmetic  33.5 us (5%)
  between operations  14.2 us (2%)
    reduce_scatter x1, waiting for transfers between devices, shards(): lax.psum_scatter(probe_acc, 'depth', scatter_dimension=1, tiled=True)  260 us
    ppermute x2, waiting for transfers between devices, with_halo(): before = lax.ppermute(last, axis, up)  86.6 us
    ppermute x18, starting transfers between devices, shifted(): return lax.ppermute(value, axis, pairs)  60.8 us
    another operation x1, loops' own time, shards(): grads = lax.fori_loop(0, order.shape[0], place_one, grads_start)  45.9 us
    ppermute x18, waiting for transfers between devices, shifted(): return lax.ppermute(value, axis, pairs)  45.2 us
    dynamic_update_slice x8, local copies, waits for them, and re-layouts, place_one(): lax.dynamic_update_slice(total, current + windows[item] * weights[item],...  32.9 us
    dot_general x80, matrix products, prod(): return jnp.einsum('...ij,jk->...ik', x, m, precision=HIGH)  25.1 us
    gather x24, local copies, waits for them, and re-layouts  24.2 us
  transfers between devices with their start and end apart: 24, of which 23 were waited for; matrix products, arithmetic and copies ran while one was open for 10% of the time, Pallas kernels for 0%

profile of v1, /device:TPU:2, one launch (start us, length us, event | category | flops | bytes accessed | tf_op | source)
XLA Modules:
  0.0 721.1 jit_solution(10650165308768826969)
XLA Ops:
  15.9 40.7 %collective-permute-done.2 = f32[2,2,64,2048]{3,2,1,0:T(8,128)S(1)} collective-permute-done((f32[2,2,64,2048]{3,2,1,0:T(8,128)}, f32[2,2,64,2048]{3,2,1,0:T(8,128)S(1)}, u32[]{:S(2)}, u32[]{:S(2)}) %collective-permute-start.2) | collective-permute-done | bytes 2097184 | tf_op jit(solution)/shard_map/ppermute | solution.py:18
  59.9 5.7 pad_maximum_fusion.2
  65.8 24.3 %while.68 = (s32[]{:T(128)}, f32[2,2,192,2048]{3,2,1,0:T(8,128)}, s32[8,4]{0,1:T(4,128)S(1)}, f32[8,2,2,128,128]{4,3,1,2,0:T(8,128)S(1)}, s32[]{:T(128)}) while((s32[]{:T(128)}, f32[2,2,192,2048]{3,2,1,0:T(8,128)}, s32[8,4]{0,1:T(4,128)S(1)}, f32[8,2,2,128,128]{4,3,1,2,0:T(8,128)S(1)}, s32[]{:T(128)}) %tuple.377), condition=%wide.while_cond.6, body=%wide.while_body.6.sunk | while | flops 2 | bytes 525937 | solution.py:119
  92.4 92.6 %while.69 = (s32[]{:T(128)}, f32[1,2,128,128]{3,2,1,0:T(8,128)S(1)}, f32[8,2,128,128]{3,2,1,0:T(8,128)}, f32[8,2,128,128]{3,2,1,0:T(8,128)}, s32[]{:T(128)}, /*i...) while((s32[]{:T(128)}, ...), condition=%wide.region_5.7_spmd.clone.clone.clone, body=%wide.region_0.6_spmd.clone.clone.clone.sunk | while | flops 1209614336 | bytes 16059241 | solution.py:190
  93.2 13.6 %conditional.12 = (f32[1,2,128,128]{3,2,1,0:T(8,128)S(1)}, f32[8,2,128,128]{3,2,1,0:T(8,128)}, f32[8,2,128,128]{3,2,1,0:T(8,128)}) conditional(s32[]{:T(128)} %bitcast.559, (f32[8,2,128,128]{3,2,1,0:T(8,128)}, f32[8,2,128,128]{3,2,1,0:T(8,128)}) %tuple.367, (s32[]{:T(128)}, s32[8]{0:T(128)S(1)}, f32[8,2,2,128,128]{4,3,1,2,0:T(8,128)S(1)}, ...), branch_computations={%region_1.1_spmd, %region_2.5_spmd.clone} | conditional | flops 1209352192 | bytes 15337401 | solution.py:183
  109.9 13.6 %conditional.12 = (f32[1,2,128,128]{3,2,1,0:T(8,128)S(1)}, f32[8,2,128,128]{3,2,1,0:T(8,128)}, f32[8,2,128,128]{3,2,1,0:T(8,128)}) conditional(s32[]{:T(128)} %bitcast.559, (f32[8,2,128,128]{3,2,1,0:T(8,128)}, f32[8,2,128,128]{3,2,1,0:T(8,128)}) %tuple.367, (s32[]{:T(128)}, s32[8]{0:T(128)S(1)}, f32[8,2,2,128,128]{4,3,1,2,0:T(8,128)S(1)}, ...), branch_computations={%region_1.1_spmd, %region_2.5_spmd.clone} | conditional | flops 1209352192 | bytes 15337401 | solution.py:183
  123.4 10.3 %collective-permute-start = (f32[1,2,128,128]{3,2,1,0:T(8,128)S(1)}, f32[1,2,128,128]{3,2,1,0:T(8,128)S(1)}, u32[]{:S(2)}, u32[]{:S(2)}) collective-permute-start(f32[1,2,128,128]{3,2,1,0:T(8,128)S(1)} %get-tuple-element.2677), channel_id=1, source_target_pairs={{0,128},{1,129},{2,130},{3,131},{4,132},{5,133},{6,134},{7,135},{8... | collective-permute-start | bytes 393224 | tf_op jit(solution)/shard_map/while/body/eval_jaxpr/ppermute | solution.py:27
  135.6 23.9 %collective-permute-start = (f32[1,2,128,128]{3,2,1,0:T(8,128)S(1)}, f32[1,2,128,128]{3,2,1,0:T(8,128)S(1)}, u32[]{:S(2)}, u32[]{:S(2)}) collective-permute-start(f32[1,2,128,128]{3,2,1,0:T(8,128)S(1)} %get-tuple-element.2677), channel_id=1, source_target_pairs={{0,128},{1,129},{2,130},{3,131},{4,132},{5,133},{6,134},{7,135},{8... | collective-permute-start | bytes 393224 | tf_op jit(solution)/shard_map/while/body/eval_jaxpr/ppermute | solution.py:27
  186.6 96.0 %while.70 = (s32[]{:T(128)}, f32[1,2,128,128]{3,2,1,0:T(8,128)S(1)}, f32[8,2,2,128,128]{4,3,1,2,0:T(8,128)}, f32[2,128,128]{2,1,0:T(8,128)S(1)}, s32[]{:T(128)},...) while((s32[]{:T(128)}, ...), condition=%wide.region_9.11_spmd.clone.clone.clone, body=%wide.region_6.10_spmd.clone.clone.clone.sunk | while | flops 1210138624 | bytes 17565816 | solution.py:230
  188.9 21.1 %collective-permute-done.1 = f32[1,2,128,128]{3,2,1,0:T(8,128)S(1)} collective-permute-done((f32[1,2,128,128]{3,2,1,0:T(8,128)S(1)}, f32[1,2,128,128]{3,2,1,0:T(8,128)S(1)}, u32[]{:S(2)}, u32[]{:S(2)}) %collective-permute-start.1) | collective-permute-done | bytes 131104 | tf_op jit(solution)/shard_map/while/body/eval_jaxpr/ppermute | solution.py:27
  210.8 20.0 %conditional.13 = (f32[1,2,128,128]{3,2,1,0:T(8,128)S(1)}, f32[8,2,2,128,128]{4,3,1,2,0:T(8,128)}, f32[2,128,128]{2,1,0:T(8,128)S(1)}) conditional(s32[]{:T(128)} %bitcast.562, (f32[8,2,2,128,128]{4,3,1,2,0:T(8,128)}, f32[2,128,128]{2,1,0:T(8,128)S(1)}) %tuple.371, (s32[]{:T(128)}, s32[8]{0:T(128)S(1)}, f32[8,2,2,128,128]{4,3,1,2,0:T(8,128)S(1)}, ...), branch_computations={%region_7.8_spmd, %region_8.9_spmd.clone} | conditional | flops 1209876480 | bytes 16843968 | solution.py:222
  234.8 20.0 %conditional.13 = (f32[1,2,128,128]{3,2,1,0:T(8,128)S(1)}, f32[8,2,2,128,128]{4,3,1,2,0:T(8,128)}, f32[2,128,128]{2,1,0:T(8,128)S(1)}) conditional(s32[]{:T(128)} %bitcast.562, (f32[8,2,2,128,128]{4,3,1,2,0:T(8,128)}, f32[2,128,128]{2,1,0:T(8,128)S(1)}) %tuple.371, (s32[]{:T(128)}, s32[8]{0:T(128)S(1)}, f32[8,2,2,128,128]{4,3,1,2,0:T(8,128)S(1)}, ...), branch_computations={%region_7.8_spmd, %region_8.9_spmd.clone} | conditional | flops 1209876480 | bytes 16843968 | solution.py:222
  283.3 259.7 %reduce-scatter.2.cloned.1.call-done = f32[2,64,128]{2,1,0:T(8,128)} async-done(((f32[2,128,128]{2,1,0:T(8,128)}), f32[2,64,128]{2,1,0:T(8,128)}) %reduce-scatter.2.cloned.1.call-update) | async-done | bytes 65552 | tf_op jit(solution)/shard_map/reduce_scatter | solution.py:248
  546.6 103.7 %while.67 = (s32[]{:T(128)}, f32[2,2,192,2048]{3,2,1,0:T(8,128)}, s32[8]{0:T(128)S(1)}, s32[8]{0:T(128)S(1)}, s32[8]{0:T(128)S(1)}, /*index=5*/f32[8,2,2,128,128...) while((s32[]{:T(128)}, f32[2,2,192,2048]{3,2,1,0:T(8,128)}, ...), condition=%wide.region_11.13_spmd, body=%wide.region_10.12_spmd.sunk | while | flops 65547 | bytes 1311491 | solution.py:242
  555.4 4.0 dynamic_update_slice.29
  568.2 4.0 dynamic_update_slice.29
  581.1 4.2 dynamic_update_slice.29
  594.1 4.0 dynamic_update_slice.29
  607.0 4.2 dynamic_update_slice.29
  620.0 4.0 dynamic_update_slice.29
  632.9 4.3 dynamic_update_slice.29
  646.0 4.2 dynamic_update_slice.29
  658.8 45.8 %collective-permute-done.4 = f32[2,2,64,2048]{3,2,1,0:T(8,128)S(1)} collective-permute-done((f32[2,2,64,2048]{3,2,1,0:T(8,128)S(1)}, f32[2,2,64,2048]{3,2,1,0:T(8,128)S(1)}, u32[]{:S(2)}, u32[]{:S(2)}) %collective-permute-start.4) | collective-permute-done | bytes 2097184 | tf_op jit(solution)/shard_map/ppermute | solution.py:18
  709.8 4.5 reduce_sum.9
  (408 shorter events, 194.5 us)
Async XLA Ops:
  7.2 535.9 %reduce-scatter.2.cloned.1.call-start = ((), (), s32[]{:S(2)}) async-start(), calls=%async_computation.1 | async-start | bytes 196608 | tf_op jit(solution)/shard_map/reduce_scatter | solution.py:248
  7.2 49.5 %collective-permute-start.2 = (f32[2,2,64,2048]{3,2,1,0:T(8,128)}, f32[2,2,64,2048]{3,2,1,0:T(8,128)S(1)}, u32[]{:S(2)}, u32[]{:S(2)}) collective-permute-start(f32[2,2,64,2048]{3,2,1,0:T(8,128)} %param.28), channel_id=1, source_target_pairs={{0,1},{1,2},{2,3},{3,4},{4,5},{5,6},{6,7},{7,8},{8,9},{9,10},{10,1... | collective-permute-start | bytes 6291464 | tf_op jit(solution)/shard_map/ppermute | solution.py:18
  10.6 49.3 %collective-permute-start.3 = (f32[2,2,64,2048]{3,2,1,0:T(8,128)}, f32[2,2,64,2048]{3,2,1,0:T(8,128)}, u32[]{:S(2)}, u32[]{:S(2)}) collective-permute-start(f32[2,2,64,2048]{3,2,1,0:T(8,128)} %param.28), channel_id=1, source_target_pairs={{1,0},{2,1},{3,2},{4,3},{5,4},{6,5},{7,6},{8,7},{9,8},{10,9},{11,1... | collective-permute-start | bytes 6291464 | tf_op jit(solution)/shard_map/ppermute | solution.py:19
  106.8 2.3 collective-permute-start
  123.4 11.3 %collective-permute-start = (f32[1,2,128,128]{3,2,1,0:T(8,128)S(1)}, f32[1,2,128,128]{3,2,1,0:T(8,128)S(1)}, u32[]{:S(2)}, u32[]{:S(2)}) collective-permute-start(f32[1,2,128,128]{3,2,1,0:T(8,128)S(1)} %get-tuple-element.2677), channel_id=1, source_target_pairs={{0,128},{1,129},{2,130},{3,131},{4,132},{5,133},{6,134},{7,135},{8... | collective-permute-start | bytes 393224 | tf_op jit(solution)/shard_map/while/body/eval_jaxpr/ppermute | solution.py:27
  135.6 24.8 %collective-permute-start = (f32[1,2,128,128]{3,2,1,0:T(8,128)S(1)}, f32[1,2,128,128]{3,2,1,0:T(8,128)S(1)}, u32[]{:S(2)}, u32[]{:S(2)}) collective-permute-start(f32[1,2,128,128]{3,2,1,0:T(8,128)S(1)} %get-tuple-element.2677), channel_id=1, source_target_pairs={{0,128},{1,129},{2,130},{3,131},{4,132},{5,133},{6,134},{7,135},{8... | collective-permute-start | bytes 393224 | tf_op jit(solution)/shard_map/while/body/eval_jaxpr/ppermute | solution.py:27
  161.3 3.2 collective-permute-start
  165.4 3.2 collective-permute-start
  169.4 3.2 collective-permute-start
  173.5 3.2 collective-permute-start
  177.6 3.2 collective-permute-start
  181.7 3.2 collective-permute-start
  187.6 22.4 %collective-permute-start.1 = (f32[1,2,128,128]{3,2,1,0:T(8,128)S(1)}, f32[1,2,128,128]{3,2,1,0:T(8,128)S(1)}, u32[]{:S(2)}, u32[]{:S(2)}) collective-permute-start(f32[1,2,128,128]{3,2,1,0:T(8,128)S(1)} %get-tuple-element.2694), channel_id=1, source_target_pairs={{128,0},{129,1},{130,2},{131,3},{132,4},{133,5},{134,6},{135,7},{1... | collective-permute-start | bytes 393224 | tf_op jit(solution)/shard_map/while/body/eval_jaxpr/ppermute | solution.py:27
  230.8 3.2 collective-permute-start.1
  254.8 3.2 collective-permute-start.1
  258.9 3.2 collective-permute-start.1
  263.0 3.2 collective-permute-start.1
  267.1 3.2 collective-permute-start.1
  271.2 3.2 collective-permute-start.1
  275.3 3.2 collective-permute-start.1
  279.4 3.2 collective-permute-start.1
  283.3 426.6 %all-gather.3.cloned.1.call-start = ((), (), s32[]{:S(2)}) async-start(), calls=%async_computation.2 | async-start | bytes 8454144 | tf_op jit(solution)/shard_map/all_gather | solution.py:249
  652.8 51.8 %collective-permute-start.4 = (f32[2,2,64,2048]{3,2,1,0:T(8,128)S(1)}, f32[2,2,64,2048]{3,2,1,0:T(8,128)S(1)}, u32[]{:S(2)}, u32[]{:S(2)}) collective-permute-start(f32[2,2,64,2048]{3,2,1,0:T(8,128)S(1)} %get-tuple-element.2463), channel_id=1, source_target_pairs={{0,1},{1,2},{2,3},{3,4},{4,5},{5,6},{6,7},{7,8},{8,9},{9,10},{10,1... | collective-permute-start | bytes 6291464 | tf_op jit(solution)/shard_map/ppermute | solution.py:18
  656.5 49.9 %collective-permute-start.5 = (f32[2,2,64,2048]{3,2,1,0:T(8,128)S(1)}, f32[2,2,64,2048]{3,2,1,0:T(8,128)S(1)}, u32[]{:S(2)}, u32[]{:S(2)}) collective-permute-start(f32[2,2,64,2048]{3,2,1,0:T(8,128)S(1)} %get-tuple-element.2464), channel_id=1, source_target_pairs={{1,0},{2,1},{3,2},{4,3},{5,4},{6,5},{7,6},{8,7},{9,8},{10,9},{11,1... | collective-permute-start | bytes 6291464 | tf_op jit(solution)/shard_map/ppermute | solution.py:19
  (3 other events, 30.7 us)
Sparse Core Ops, SparseCore 0:
  283.4 259.5 reduce-scatter.1
  546.6 125.2 all-gather.2
